TPU v7x, 32 devices: a whole 2x2x4 slice. The times are simulated.
32 devices in a mesh: rep: 2 (over core), shard: 16 (over z, y, x).
Axes of the slice: x: 2, y: 2, z: 4, core: 2. Of those that a mesh axis runs over, the one named last changes fastest.
Arguments:
- tokens: bfloat16 [32, 1024, 768], P('rep', 'shard'), may hold values from -6 to 6
- cotangent: bfloat16 [32, 1024, 768], P('rep', 'shard'), may hold values from -6 to 6
- lengths: int32 [2, 16], P('rep'), may hold values from 512 to 1024, as said below
- order: int32 [2, 16], P('rep'), may hold values from 0 to 15, each once within a row
- norm_weight: bfloat16 [768], P('shard'), may hold values from 0.099609375 to 1.8984375
- in_weight: bfloat16 [768, 3352], P('shard'), may hold values from -0.21875 to 0.21875
- conv_weight: bfloat16 [1792, 4], P('shard'), may hold values from -3 to 3
- conv_bias: bfloat16 [1792], P('shard'), may hold values from -3 to 3
- step_bias: float32 [24], replicated, may hold values from -5.5 to -2.5
- decay_log: float32 [24], replicated, may hold values from 0 to 2.77
- skip_gain: float32 [24], replicated, may hold values from 0.5 to 1.5
- gate_norm_weight: bfloat16 [1536], P('shard'), may hold values from 0.099609375 to 1.8984375
- out_weight: bfloat16 [1536, 768], P('shard'), may hold values from -0.15625 to 0.15625
Outputs:
- output: bfloat16 [32, 1024, 768], P('rep', 'shard')
- input_grad: bfloat16 [32, 1024, 768], P('rep', 'shard')
- grad_norm: float32 [768], P('shard')
- grad_in: float32 [768, 3352], P('shard')
- grad_conv: float32 [1792, 4], P('shard')
- grad_conv_bias: float32 [1792], P('shard')
- grad_step_bias: float32 [24], replicated
- grad_decay_log: float32 [24], replicated
- grad_skip: float32 [24], replicated
- grad_gate_norm: float32 [1536], P('shard')
- grad_out: float32 [1536, 768], P('shard')
Inputs may be any that keep to these rules, and one draw needn't show every extreme that they name: Each row of order holds every number from 0 to 15 once: slot k of group r holds sequence order[r, k]. lengths[r, s] counts the valid leading positions of sequence s of group r; each row has one entry equal to 1024 and one equal to 512.
All inputs are finite; a program needn't handle non-finite values.
Results may differ from a plain program's by a relative error of at most 0.012.
The roundings to bfloat16 on the way count: a program that leaves them out, or rounds other values in their place, can miss the bound.
Values may be sent and summed in bfloat16 or wider, within the bound.
A program may use at most 192 MiB of HBM per device.

v0:
```python
import jax
import jax.numpy as jnp
from jax import lax
from jax.sharding import PartitionSpec as P

HEADS = 24
HEADDIM = 64
STATE = 128
CONV = 4
SPAN = 256
DI = 1536
XBC = 1792
epsilon = 1e-05


def decay_terms(log_block, step_block):
    cumul = jnp.cumsum(log_block, axis=0)
    cumul_heads = cumul.T
    positions = log_block.shape[0]
    causal = jnp.arange(positions)[:, None] >= jnp.arange(positions)[None, :]
    spread = jnp.where(causal[None], cumul_heads[:, :, None] - cumul_heads[:, None, :], 0.0)
    factor = jnp.where(causal[None], jnp.exp(spread), 0.0) * step_block.T[:, None, :]
    carry_weight = jnp.exp(cumul[-1][None, :] - cumul) * step_block
    return (factor, carry_weight, jnp.exp(cumul), jnp.exp(cumul[-1]))


def norm_part(tok_float, norm_gain):
    return (
        tok_float
        * lax.rsqrt(jnp.mean(tok_float * tok_float, axis=-1, keepdims=True) + epsilon)
        * norm_gain
    )


def conv_part(conv_in, conv_taps, conv_shift):
    length = conv_in.shape[0]
    padded = jnp.concatenate(
        [jnp.zeros((CONV - 1, conv_in.shape[1]), jnp.float32), conv_in], axis=0
    )
    total = conv_shift[None, :] + jnp.zeros_like(conv_in)
    for tap in range(CONV):
        total = total + conv_taps[:, tap][None, :] * padded[tap : tap + length]
    return jax.nn.silu(total)


def step_part(step_raw, step_bias, decay_log):
    step_size = jax.nn.softplus(step_raw + step_bias[None, :])
    return (step_size, -jnp.exp(decay_log)[None, :] * step_size)


def gate_part(scan_out, heads_in, skip_gain, gate_raw, gate_gain):
    mixed = scan_out + jnp.repeat(skip_gain, HEADDIM)[None, :] * heads_in
    gated = mixed * jax.nn.silu(gate_raw)
    return gated * lax.rsqrt(jnp.mean(gated * gated, axis=-1, keepdims=True) + epsilon) * gate_gain


def block_forward(state, inputs):
    heads_blk, keys_blk, query_blk, step_blk, log_blk = inputs
    factor, carry_weight, growth, growth_last = decay_terms(log_blk, step_blk)
    scores = jnp.einsum("tn,sn->ts", query_blk, keys_blk, preferred_element_type=jnp.float32)
    mixing = (scores[None] * factor).astype(jnp.bfloat16)
    within = jnp.einsum("hts,shp->thp", mixing, heads_blk, preferred_element_type=jnp.float32)
    across = jnp.einsum(
        "tn,hpn->thp", query_blk, state.astype(jnp.bfloat16), preferred_element_type=jnp.float32
    )
    result = within + growth[:, :, None] * across
    weighted = (heads_blk.astype(jnp.float32) * carry_weight[:, :, None]).astype(jnp.bfloat16)
    contrib = jnp.einsum("sn,shp->hpn", keys_blk, weighted, preferred_element_type=jnp.float32)
    return (growth_last[:, None, None] * state + contrib, (result, state))


def block_backward(later, inputs):
    heads_blk, keys_blk, query_blk, step_blk, log_blk, grad_blk, state = inputs
    terms, decay_pull = jax.vjp(decay_terms, log_blk, step_blk)
    factor, carry_weight, growth, growth_last = terms
    scores = jnp.einsum("tn,sn->ts", query_blk, keys_blk, preferred_element_type=jnp.float32)
    mixing = (scores[None] * factor).astype(jnp.bfloat16)
    state_low = state.astype(jnp.bfloat16)
    across = jnp.einsum("tn,hpn->thp", query_blk, state_low, preferred_element_type=jnp.float32)
    heads_float = heads_blk.astype(jnp.float32)
    weighted = (heads_float * carry_weight[:, :, None]).astype(jnp.bfloat16)
    grad_within = grad_blk.astype(jnp.bfloat16)
    grad_across = (growth[:, :, None] * grad_blk).astype(jnp.bfloat16)
    grad_mixing = jnp.einsum(
        "thp,shp->hts", grad_within, heads_blk, preferred_element_type=jnp.float32
    )
    grad_heads = jnp.einsum("hts,thp->shp", mixing, grad_within, preferred_element_type=jnp.float32)
    grad_query = jnp.einsum(
        "thp,hpn->tn", grad_across, state_low, preferred_element_type=jnp.float32
    )
    grad_state = jnp.einsum(
        "thp,tn->hpn", grad_across, query_blk, preferred_element_type=jnp.float32
    )
    grad_state = grad_state + growth_last[:, None, None] * later
    grad_growth = jnp.sum(grad_blk * across, axis=2)
    later_low = later.astype(jnp.bfloat16)
    grad_weighted = jnp.einsum(
        "hpn,sn->shp", later_low, keys_blk, preferred_element_type=jnp.float32
    )
    grad_keys = jnp.einsum("hpn,shp->sn", later_low, weighted, preferred_element_type=jnp.float32)
    grad_heads = grad_heads + grad_weighted * carry_weight[:, :, None]
    grad_carry = jnp.sum(grad_weighted * heads_float, axis=2)
    grad_last = jnp.sum(later * state, axis=(1, 2))
    grad_scores = jnp.sum(grad_mixing * factor, axis=0).astype(jnp.bfloat16)
    grad_query = grad_query + jnp.dot(grad_scores, keys_blk, preferred_element_type=jnp.float32)
    grad_keys = grad_keys + jnp.einsum(
        "ts,tn->sn", grad_scores, query_blk, preferred_element_type=jnp.float32
    )
    grad_log, grad_step = decay_pull(
        (grad_mixing * scores[None], grad_carry, grad_growth, grad_last)
    )
    return (grad_state, (grad_heads, grad_keys, grad_query, grad_step, grad_log))


def forward_seq(
    tok_float,
    keep,
    norm_full,
    in_full,
    conv_full,
    shift_full,
    gate_full,
    out_full,
    step_bias,
    decay_log,
    skip_gain,
):
    seq_len = tok_float.shape[0]
    normed, norm_pull = jax.vjp(norm_part, tok_float, norm_full.astype(jnp.float32))
    normed_low = normed.astype(jnp.bfloat16)
    projected = jnp.dot(normed_low, in_full, preferred_element_type=jnp.float32)
    gate_raw = projected[:, :DI]
    conv_in = projected[:, DI : DI + XBC]
    step_raw = projected[:, DI + XBC :]
    convolved, conv_pull = jax.vjp(
        conv_part, conv_in, conv_full.astype(jnp.float32), shift_full.astype(jnp.float32)
    )
    heads_in = convolved[:, :DI]
    heads_low = heads_in.astype(jnp.bfloat16)
    key_low = convolved[:, DI : DI + STATE].astype(jnp.bfloat16)
    query_low = convolved[:, DI + STATE :].astype(jnp.bfloat16)
    decays, step_pull = jax.vjp(step_part, step_raw, step_bias, decay_log)
    step_size, log_decay = decays
    count = seq_len // SPAN
    blocks = (
        heads_low.reshape(count, SPAN, HEADS, HEADDIM),
        key_low.reshape(count, SPAN, STATE),
        query_low.reshape(count, SPAN, STATE),
        step_size.reshape(count, SPAN, HEADS),
        log_decay.reshape(count, SPAN, HEADS),
    )
    start = jnp.zeros((HEADS, HEADDIM, STATE), jnp.float32)
    final_state, kept = lax.scan(block_forward, start, blocks)
    scan_blocks, states = kept
    scan_out = scan_blocks.reshape(seq_len, DI)
    gate_value, gate_pull = jax.vjp(
        gate_part, scan_out, heads_in, skip_gain, gate_raw, gate_full.astype(jnp.float32)
    )
    gate_low = gate_value.astype(jnp.bfloat16)
    branch = jnp.dot(gate_low, out_full, preferred_element_type=jnp.float32)
    result = (tok_float + keep[:, None] * branch).astype(jnp.bfloat16)
    saved = (keep, normed_low, norm_pull, conv_pull, step_pull, gate_pull, gate_low, blocks, states)
    return (result, saved)


def backward_seq(saved, cot_float, in_full, out_full):
    keep, normed_low, norm_pull, conv_pull, step_pull, gate_pull, gate_low, blocks, states = saved
    seq_len = cot_float.shape[0]
    count = seq_len // SPAN
    grad_branch = (keep[:, None] * cot_float).astype(jnp.bfloat16)
    grad_out_full = jnp.einsum(
        "ti,tj->ij", gate_low, grad_branch, preferred_element_type=jnp.float32
    )
    grad_gate = jnp.einsum("tj,ij->ti", grad_branch, out_full, preferred_element_type=jnp.float32)
    grad_scan, grad_heads_skip, grad_skip, grad_gate_raw, grad_gate_gain = gate_pull(grad_gate)
    grad_scan_blocks = grad_scan.reshape(count, SPAN, HEADS, HEADDIM)
    first_grad, grads = lax.scan(
        block_backward,
        jnp.zeros((HEADS, HEADDIM, STATE), jnp.float32),
        (blocks[0], blocks[1], blocks[2], blocks[3], blocks[4], grad_scan_blocks, states),
        reverse=True,
    )
    grad_heads, grad_keys, grad_query, grad_step, grad_log = grads
    grad_step_raw, grad_step_bias, grad_decay_log = step_pull(
        (grad_step.reshape(seq_len, HEADS), grad_log.reshape(seq_len, HEADS))
    )
    grad_convolved = jnp.concatenate(
        [
            grad_heads.reshape(seq_len, DI) + grad_heads_skip,
            grad_keys.reshape(seq_len, STATE),
            grad_query.reshape(seq_len, STATE),
        ],
        axis=1,
    )
    grad_conv_in, grad_taps, grad_shift = conv_pull(grad_convolved)
    grad_projected = jnp.concatenate([grad_gate_raw, grad_conv_in, grad_step_raw], axis=1).astype(
        jnp.bfloat16
    )
    grad_in_full = jnp.einsum(
        "ti,tj->ij", normed_low, grad_projected, preferred_element_type=jnp.float32
    )
    grad_normed = jnp.einsum(
        "tj,ij->ti", grad_projected, in_full, preferred_element_type=jnp.float32
    )
    grad_tok, grad_norm_gain = norm_pull(grad_normed)
    input_grad = (cot_float + grad_tok).astype(jnp.bfloat16)
    weight_grads = (
        grad_norm_gain,
        grad_in_full,
        grad_taps,
        grad_shift,
        grad_gate_gain,
        grad_out_full,
    )
    return (input_grad, weight_grads, (grad_step_bias, grad_decay_log, grad_skip))


def on_device(
    tokens,
    cotangent,
    lengths,
    order,
    norm_weight,
    in_weight,
    conv_weight,
    conv_bias,
    step_bias,
    decay_log,
    skip_gain,
    gate_norm_weight,
    out_weight,
):
    peers = lax.axis_size("shard")
    rank = lax.axis_index("shard")
    slots = jnp.arange(peers, dtype=jnp.int32)
    order_row = order[0]
    inverse = jnp.sum(jnp.where(order_row[None, :] == slots[:, None], slots[None, :], 0), axis=1)
    piece = tokens.shape[1]
    width = tokens.shape[2]
    sent_tokens = jnp.take(tokens, inverse, axis=0).reshape(peers, 1, piece, width)
    sent_cot = jnp.take(cotangent, inverse, axis=0).reshape(peers, 1, piece, width)
    got_tokens, got_cot = (
        lax.all_to_all(sent_tokens, "shard", split_axis=0, concat_axis=2, tiled=True),
        lax.all_to_all(sent_cot, "shard", split_axis=0, concat_axis=2, tiled=True),
    )
    seq_len = got_tokens.shape[2]
    length_row = lengths[0]
    gathered = (
        lax.all_gather(norm_weight, "shard", axis=0, tiled=True),
        lax.all_gather(in_weight, "shard", axis=0, tiled=True),
        lax.all_gather(conv_weight, "shard", axis=0, tiled=True),
        lax.all_gather(conv_bias, "shard", axis=0, tiled=True),
        lax.all_gather(gate_norm_weight, "shard", axis=0, tiled=True),
        lax.all_gather(out_weight, "shard", axis=0, tiled=True),
    )
    norm_full, in_full, conv_full, shift_full, gate_full, out_full = gathered
    valid = length_row[rank]
    keep = (jnp.arange(seq_len, dtype=jnp.int32) < valid).astype(jnp.float32)
    forward_out, saved = forward_seq(
        got_tokens[0, 0].astype(jnp.float32),
        keep,
        norm_full,
        in_full,
        conv_full,
        shift_full,
        gate_full,
        out_full,
        step_bias,
        decay_log,
        skip_gain,
    )
    result = forward_out[None]
    grad_seq, weight_grads, head_terms = backward_seq(
        saved, got_cot[0, 0].astype(jnp.float32), in_full, out_full
    )
    input_grad = grad_seq[None]
    back_out, back_grad = (
        lax.all_to_all(result, "shard", split_axis=1, concat_axis=0, tiled=True),
        lax.all_to_all(input_grad, "shard", split_axis=1, concat_axis=0, tiled=True),
    )
    output = jnp.take(back_out, order_row, axis=0)
    input_back = jnp.take(back_grad, order_row, axis=0)
    summed = lax.psum(
        (
            weight_grads[0],
            weight_grads[1],
            weight_grads[2],
            weight_grads[3],
            weight_grads[4],
            weight_grads[5],
        ),
        "rep",
    )
    pieces = (
        lax.psum_scatter(summed[0], "shard", scatter_dimension=0, tiled=True),
        lax.psum_scatter(summed[1], "shard", scatter_dimension=0, tiled=True),
        lax.psum_scatter(summed[2], "shard", scatter_dimension=0, tiled=True),
        lax.psum_scatter(summed[3], "shard", scatter_dimension=0, tiled=True),
        lax.psum_scatter(summed[4], "shard", scatter_dimension=0, tiled=True),
        lax.psum_scatter(summed[5], "shard", scatter_dimension=0, tiled=True),
    )
    head_sums = lax.psum((head_terms[0], head_terms[1], head_terms[2]), ("rep", "shard"))
    return (
        output,
        input_back,
        pieces[0],
        pieces[1],
        pieces[2],
        pieces[3],
        head_sums[0],
        head_sums[1],
        head_sums[2],
        pieces[4],
        pieces[5],
    )


def solution(mesh):
    placed = (
        P("rep", "shard", None),
        P("rep", "shard", None),
        P("rep", None),
        P("rep", None),
        P("shard"),
        P("shard", None),
        P("shard", None),
        P("shard"),
        P(),
        P(),
        P(),
        P("shard"),
        P("shard", None),
    )
    return jax.shard_map(
        on_device,
        mesh=mesh,
        in_specs=placed,
        out_specs=(
            P("rep", "shard", None),
            P("rep", "shard", None),
            P("shard"),
            P("shard", None),
            P("shard", None),
            P("shard"),
            P(),
            P(),
            P(),
            P("shard"),
            P("shard", None),
        ),
        check_vma=False,
    )
```

profile of v0, /device:TPU:0, one launch (start us, length us, event | category | flops | bytes accessed | tf_op | source)
XLA Modules:
  0.0 1286.4 jit_solution(3603219273039151114)
XLA Ops:
  15.6 65.5 %all_to_all.42 = bf16[16,1,64,768]{3,2,1,0:T(8,128)(2,1)S(1)} all-to-all(bf16[16,1,64,768]{3,2,1,0:T(8,128)(2,1)S(1)} %get-tuple-element.698), channel_id=1, replica_groups=mesh['rep'=2,'shard'=16] {'shard'}, dimensions={0} | all-to-all | bytes 3145728 | tf_op jit(solution)/shard_map/all_to_all | solution.py:243
  89.8 115.9 %all-reduce.21 = (bf16[768]{0:T(1024)(128)(2,1)S(1)}, bf16[1792]{0:T(1024)(128)(2,1)S(1)}, bf16[1536]{0:T(1024)(128)(2,1)S(1)}) all-reduce(bf16[768]{0:T(1024)(128)(2,1)S(1)} %dynamic-update-slice, bf16[1792]{0:T(1024)(128)(2,1)S(1)} %dynamic-update-slice.1, ...), channel_id=1, replica_groups=mesh['rep'=2,'shard'=16] {'shard'}, use_global_device_ids=true, to_apply=%add.11 | all-reduce | flops 4096 | bytes 16384
  205.8 35.7 %all-gather = bf16[16,112,4]{1,2,0:T(4,128)(2,1)S(1)} all-gather(bf16[1,112,4]{1,2,0:T(4,128)(2,1)S(1)} %bitcast.455), channel_id=1, replica_groups=mesh['rep'=2,'shard'=16] {'shard'}, dimensions={0}, use_global_device_ids=true | all-gather | bytes 15232 | tf_op jit(solution)/shard_map/all_gather | solution.py:251
  297.2 182.0 %while.40 = (s32[]{:T(128)}, f32[24,64,128]{2,1,0:T(8,128)S(1)}, f32[4,256,24,64]{1,0,3,2:T(4,128)}, f32[4,24,64,128]{3,2,1,0:T(8,128)}, f32[4,256,24]{1,2,0:T(8...) while((s32[]{:T(128)}, f32[24,64,128]{2,1,0:T(8,128)S(1)}, ...), condition=%wide.region_5.7_spmd.clone, body=%wide.region_2.0_spmd.clone.sunk | while | flops 432687168 | bytes 17880888 | solution.py:153
  305.7 34.5 %dynamic_update_slice.73 = f32[4,256,24,64]{1,0,3,2:T(4,128)} dynamic-update-slice(f32[4,256,24,64]{1,0,3,2:T(4,128)} %get-tuple-element.896, f32[1,256,24,64]{1,0,3,2:T(1,128)S(1)} %copy.355, s32[]{:T(128)} %get-tuple-element.894, s32[]{:T(128)} %constant.126.clone.1..sunk, s32[]{:T(128)} %constant.126.clone.1..sunk, s32[]{:T(128)} %constant.126.clone.1..sunk) | dynamic-update-slice | bytes 3145732 | tf_op jit(solution)/shard_map/while/body/jit(dynamic_update_index_in_dim)/dynamic_update_slice | solution.py:153
  351.2 34.5 %dynamic_update_slice.73 = f32[4,256,24,64]{1,0,3,2:T(4,128)} dynamic-update-slice(f32[4,256,24,64]{1,0,3,2:T(4,128)} %get-tuple-element.896, f32[1,256,24,64]{1,0,3,2:T(1,128)S(1)} %copy.355, s32[]{:T(128)} %get-tuple-element.894, s32[]{:T(128)} %constant.126.clone.1..sunk, s32[]{:T(128)} %constant.126.clone.1..sunk, s32[]{:T(128)} %constant.126.clone.1..sunk) | dynamic-update-slice | bytes 3145732 | tf_op jit(solution)/shard_map/while/body/jit(dynamic_update_index_in_dim)/dynamic_update_slice | solution.py:153
  396.6 34.5 %dynamic_update_slice.73 = f32[4,256,24,64]{1,0,3,2:T(4,128)} dynamic-update-slice(f32[4,256,24,64]{1,0,3,2:T(4,128)} %get-tuple-element.896, f32[1,256,24,64]{1,0,3,2:T(1,128)S(1)} %copy.355, s32[]{:T(128)} %get-tuple-element.894, s32[]{:T(128)} %constant.126.clone.1..sunk, s32[]{:T(128)} %constant.126.clone.1..sunk, s32[]{:T(128)} %constant.126.clone.1..sunk) | dynamic-update-slice | bytes 3145732 | tf_op jit(solution)/shard_map/while/body/jit(dynamic_update_index_in_dim)/dynamic_update_slice | solution.py:153
  442.1 34.5 %dynamic_update_slice.73 = f32[4,256,24,64]{1,0,3,2:T(4,128)} dynamic-update-slice(f32[4,256,24,64]{1,0,3,2:T(4,128)} %get-tuple-element.896, f32[1,256,24,64]{1,0,3,2:T(1,128)S(1)} %copy.355, s32[]{:T(128)} %get-tuple-element.894, s32[]{:T(128)} %constant.126.clone.1..sunk, s32[]{:T(128)} %constant.126.clone.1..sunk, s32[]{:T(128)} %constant.126.clone.1..sunk) | dynamic-update-slice | bytes 3145732 | tf_op jit(solution)/shard_map/while/body/jit(dynamic_update_index_in_dim)/dynamic_update_slice | solution.py:153
  506.9 14.3 %multiply_reduce_fusion.7 = (f32[1536]{0:T(1024)}, f32[1024,1536]{0,1:T(8,128)}, bf16[1024,1536]{0,1:T(8,128)(2,1)}) fusion(f32[1024,1792]{0,1:T(8,128)} %copy-done.2, f32[1024,3352]{0,1:T(8,128)} %fusion.140, f32[1024,1536]{0,1:T(8,128)S(1)} %copy-done.8, f32[1024]{0:T(1024)S(1)} %multiply_multiply_fusion.1, f32[1024]{0:T(1024)S(1)} %fusion.127, ...), kind=kLoop, calls=%fused_computation.179 | loop fusion | flops 34601472 | bytes 40921088 | tf_op jit(solution)/shard_map/transpose(jvp())/reduce_sum | solution.py:52
  536.4 292.3 %while.41 = (s32[]{:T(128)}, f32[24,64,128]{2,1,0:T(8,128)S(1)}, f32[4,256,24,64]{1,0,3,2:T(4,128)}, f32[4,256,128]{2,1,0:T(8,128)}, f32[4,256,128]{2,1,0:T(8,12...) while((s32[]{:T(128)}, f32[24,64,128]{2,1,0:T(8,128)S(1)}, ...), condition=%wide.region_21.23_spmd.clone, body=%wide.region_8.22_spmd.clone.sunk | while | flops 998139968 | bytes 33770432 | solution.py:177
  562.6 34.8 %dynamic_update_slice.76 = f32[4,256,24,64]{1,0,3,2:T(4,128)} dynamic-update-slice(f32[4,256,24,64]{1,0,3,2:T(4,128)} %get-tuple-element.938, f32[1,256,24,64]{1,0,3,2:T(1,128)} %copy.368, s32[]{:T(128)S(6)} %sub.232, s32[]{:T(128)} %constant.126.clone.1..sunk.1, s32[]{:T(128)} %constant.126.clone.1..sunk.1, s32[]{:T(128)} %constant.126.clone.1..sunk.1) | dynamic-update-slice | bytes 3145732 | tf_op jit(solution)/shard_map/while/body/jit(dynamic_update_index_in_dim)/dynamic_update_slice | solution.py:153
  635.7 34.7 %dynamic_update_slice.76 = f32[4,256,24,64]{1,0,3,2:T(4,128)} dynamic-update-slice(f32[4,256,24,64]{1,0,3,2:T(4,128)} %get-tuple-element.938, f32[1,256,24,64]{1,0,3,2:T(1,128)} %copy.368, s32[]{:T(128)S(6)} %sub.232, s32[]{:T(128)} %constant.126.clone.1..sunk.1, s32[]{:T(128)} %constant.126.clone.1..sunk.1, s32[]{:T(128)} %constant.126.clone.1..sunk.1) | dynamic-update-slice | bytes 3145732 | tf_op jit(solution)/shard_map/while/body/jit(dynamic_update_index_in_dim)/dynamic_update_slice | solution.py:153
  708.7 34.7 %dynamic_update_slice.76 = f32[4,256,24,64]{1,0,3,2:T(4,128)} dynamic-update-slice(f32[4,256,24,64]{1,0,3,2:T(4,128)} %get-tuple-element.938, f32[1,256,24,64]{1,0,3,2:T(1,128)} %copy.368, s32[]{:T(128)S(6)} %sub.232, s32[]{:T(128)} %constant.126.clone.1..sunk.1, s32[]{:T(128)} %constant.126.clone.1..sunk.1, s32[]{:T(128)} %constant.126.clone.1..sunk.1) | dynamic-update-slice | bytes 3145732 | tf_op jit(solution)/shard_map/while/body/jit(dynamic_update_index_in_dim)/dynamic_update_slice | solution.py:153
  781.7 34.7 %dynamic_update_slice.76 = f32[4,256,24,64]{1,0,3,2:T(4,128)} dynamic-update-slice(f32[4,256,24,64]{1,0,3,2:T(4,128)} %get-tuple-element.938, f32[1,256,24,64]{1,0,3,2:T(1,128)} %copy.368, s32[]{:T(128)S(6)} %sub.232, s32[]{:T(128)} %constant.126.clone.1..sunk.1, s32[]{:T(128)} %constant.126.clone.1..sunk.1, s32[]{:T(128)} %constant.126.clone.1..sunk.1) | dynamic-update-slice | bytes 3145732 | tf_op jit(solution)/shard_map/while/body/jit(dynamic_update_index_in_dim)/dynamic_update_slice | solution.py:153
  844.6 19.0 %multiply_reduce_fusion.4 = (f32[1792]{0:T(1024)S(1)}, f32[1792]{0:T(1024)S(1)}, f32[1792]{0:T(1024)S(1)}, f32[1792]{0:T(1024)S(1)}, f32[1792]{0:T(1024)S(1)}, /*index=5*/f32[1024,1792]{0,1:T(8,128)S(1)}) fusion(f32[1024,1792]{0,1:T(8,128)} %copy-done.3, f32[1024,3352]{0,1:T(8,128)} %fusion.140, f32[1024,1792]{0,1:T(8,128)} %get-tuple-element.668, ...), kind=kLoop, calls=%fused_computation.169 | loop fusion | flops 36691200 | bytes 36736000 | tf_op jit(solution)/shard_map/transpose(jvp())/reduce_sum | solution.py:42
  872.1 12.1 fusion.103
  884.3 12.9 %fusion.119 = f32[768,3352]{1,0:T(8,128)} fusion(bf16[1024,768]{1,0:T(8,128)(2,1)S(1)} %copy-done.11, bf16[1024,24]{0,1:T(8,128)(2,1)S(1)} %get-tuple-element.662, bf16[1024,1792]{0,1:T(8,128)(2,1)} %fusion.103, bf16[1024,1536]{0,1:T(8,128)(2,1)} %get-tuple-element.685), kind=kOutput, calls=%fused_computation.210 | convolution fusion | flops 5292834816 | bytes 18735104 | tf_op jit(solution)/shard_map/ti,tj->ij/dot_general | solution.py:199
  909.6 11.7 reduce.22
  943.6 11.5 reduce.21
  956.5 20.8 %all-to-all-done.1 = bf16[16,2,24576]{2,1,0:T(2,128)(2,1)S(1)} async-done(((bf16[16,2,24576]{2,1,0:T(2,128)(2,1)}), bf16[16,2,24576]{2,1,0:T(2,128)(2,1)S(1)}, u32[]{:S(2)}, u32[]{:S(2)}) %all-to-all-start.1) | async-done | bytes 1572896 | tf_op jit(solution)/shard_map/all_to_all | solution.py:278
  977.2 27.4 %all-to-all-start.3 = ((bf16[16,2,24576]{2,1,0:T(2,128)(2,1)}), bf16[16,2,24576]{2,1,0:T(2,128)(2,1)S(1)}, u32[]{:S(2)}, u32[]{:S(2)}) async-start(bf16[16,2,24576]{2,1,0:T(2,128)(2,1)} %reshape.519), calls=%async_computation.3 | async-start | bytes 3145728 | tf_op jit(solution)/shard_map/all_to_all | solution.py:279
  1008.1 122.2 %reduce-scatter.6.cloned.1.call-done = f32[48,3352]{1,0:T(8,128)} async-done(((f32[768,3352]{1,0:T(8,128)}), f32[48,3352]{1,0:T(8,128)}) %reduce-scatter.6.cloned.1.call-update) | async-done | bytes 643600 | tf_op jit(solution)/shard_map/reduce_scatter | solution.py:296
  1130.6 40.0 %all-reduce.17 = (f32[24]{0:T(128)}, f32[24]{0:T(128)}, f32[24]{0:T(128)}) all-reduce(f32[24]{0:T(128)S(1)} %get-tuple-element.661, f32[24]{0:T(128)S(1)} %negate_multiply_fusion, f32[24]{0:T(128)S(1)} %reduce_sum.344), channel_id=1, replica_groups=mesh['rep'=2,'shard'=16] {'rep','shard'}, use_global_device_ids=true, to_apply=%region_38.40 | all-reduce | flops 72 | bytes 576 | tf_op jit(solution)/shard_map/psum | solution.py:302
  1170.6 75.7 %all-reduce.18 = (f32[768]{0:T(1024)S(1)}, f32[1792]{0:T(1024)S(1)}, f32[1536]{0:T(1024)S(1)}) all-reduce(f32[768]{0:T(1024)S(1)} %get-tuple-element.592, f32[1792]{0:T(1024)S(1)} %get-tuple-element.590, f32[1536]{0:T(1024)S(1)} %copy-done.36), channel_id=2, replica_groups=mesh['rep'=2,'shard'=16] {'shard'}, use_global_device_ids=true, to_apply=%region_25.27.clone | all-reduce | flops 4096 | bytes 32768
  (440 shorter events, 404.4 us)
Async XLA Ops:
  7.2 240.9 %all-gather.4.cloned.1.call-start = ((), (), s32[]{:S(2)}) async-start(), calls=%async_computation.7 | async-start | bytes 5640192 | tf_op jit(solution)/shard_map/all_gather | solution.py:250
  12.6 73.9 %copy-start.41 = (u32[32]{0:T(128)S(1)}, u32[32]{0:T(128)}, u32[]{:S(2)}) copy-start(u32[32]{0:T(128)} %constant.162) | copy-start | bytes 388
  12.6 76.5 %copy-start.44 = (bf16[112]{0:T(256)(128)(2,1)S(1)}, bf16[112]{0:T(256)(128)(2,1)}, u32[]{:S(2)}) copy-start(bf16[112]{0:T(256)(128)(2,1)} %param.26) | copy-start | bytes 676
  12.6 76.7 %copy-start.45 = (bf16[96]{0:T(256)(128)(2,1)S(1)}, bf16[96]{0:T(256)(128)(2,1)}, u32[]{:S(2)}) copy-start(bf16[96]{0:T(256)(128)(2,1)} %param.30) | copy-start | bytes 580
  12.6 77.0 %copy-start.46 = (bf16[48]{0:T(256)(128)(2,1)S(1)}, bf16[48]{0:T(256)(128)(2,1)}, u32[]{:S(2)}) copy-start(bf16[48]{0:T(256)(128)(2,1)} %param.23) | copy-start | bytes 292
  12.6 193.1 %copy-start.42 = (bf16[112,4]{0,1:T(4,128)(2,1)S(1)}, bf16[112,4]{0,1:T(4,128)(2,1)}, u32[]{:S(2)}) copy-start(bf16[112,4]{0,1:T(4,128)(2,1)} %param.25) | copy-start | bytes 2692
  12.6 228.9 %copy-start.43 = (f32[24]{0:T(128)S(1)}, f32[24]{0:T(128)}, u32[]{:S(2)}) copy-start(f32[24]{0:T(128)} %param.29) | copy-start | bytes 292
  12.7 229.0 %copy-start.47 = (s32[1,16]{1,0:T(1,128)S(1)}, s32[1,16]{1,0:T(1,128)}, u32[]{:S(2)}) copy-start(s32[1,16]{1,0:T(1,128)} %param.21) | copy-start | bytes 196
  12.7 230.4 %copy-start.49 = (f32[24]{0:T(128)S(1)}, f32[24]{0:T(128)}, u32[]{:S(2)}) copy-start(f32[24]{0:T(128)} %param.28) | copy-start | bytes 292
  81.1 178.3 %copy-start.5 = (bf16[16,1,64,768]{3,2,1,0:T(8,128)(2,1)}, bf16[16,1,64,768]{3,2,1,0:T(8,128)(2,1)S(1)}, u32[]{:S(2)}) copy-start(bf16[16,1,64,768]{3,2,1,0:T(8,128)(2,1)S(1)} %all_to_all.42) | copy-start | bytes 4718596
  81.1 164.1 %all-to-all-start.2 = ((bf16[16,1,64,768]{3,2,1,0:T(8,128)(2,1)}), bf16[16,1,64,768]{3,2,1,0:T(8,128)(2,1)}, u32[]{:S(2)}, u32[]{:S(2)}) async-start(bf16[16,1,64,768]{3,2,1,0:T(8,128)(2,1)} %get-tuple-element.697), calls=%async_computation.2 | async-start | bytes 3145728 | tf_op jit(solution)/shard_map/all_to_all | solution.py:244
  85.6 413.4 %all-gather.6.cloned.1.call-start = ((), (), s32[]{:S(2)}) async-start(), calls=%async_computation.8 | async-start | bytes 2506752 | tf_op jit(solution)/shard_map/all_gather | solution.py:254
  86.4 921.7 %reduce-scatter.8.cloned.1.call-start = ((), (), s32[]{:S(2)}) async-start(), calls=%async_computation.10 | async-start | bytes 5013504 | tf_op jit(solution)/shard_map/reduce_scatter | solution.py:300
  205.8 53.7 %copy-start.23 = (f32[768]{0:T(1024)}, f32[768]{0:T(1024)S(1)}, u32[]{:S(2)}) copy-start(f32[768]{0:T(1024)S(1)} %convert_element_type.160) | copy-start | bytes 9220
  241.7 265.1 %copy-start.29 = (f32[1536]{0:T(1024)}, f32[1536]{0:T(1024)S(1)}, u32[]{:S(2)}) copy-start(f32[1536]{0:T(1024)S(1)} %convert_element_type.165) | copy-start | bytes 18436
  529.3 601.0 %reduce-scatter.6.cloned.1.call-start = ((), (), s32[]{:S(2)}) async-start(), calls=%async_computation.9 | async-start | bytes 11280384 | tf_op jit(solution)/shard_map/reduce_scatter | solution.py:296
  922.6 54.6 %all-to-all-start.1 = ((bf16[16,2,24576]{2,1,0:T(2,128)(2,1)}), bf16[16,2,24576]{2,1,0:T(2,128)(2,1)S(1)}, u32[]{:S(2)}, u32[]{:S(2)}) async-start(bf16[16,2,24576]{2,1,0:T(2,128)(2,1)} %reshape.517), calls=%async_computation.1 | async-start | bytes 3145728 | tf_op jit(solution)/shard_map/all_to_all | solution.py:278
  943.6 62.5 %copy-start.48 = (s32[1,16]{1,0:T(1,128)S(1)}, s32[1,16]{1,0:T(1,128)}, u32[]{:S(2)}) copy-start(s32[1,16]{1,0:T(1,128)} %param.22) | copy-start | bytes 196
  943.6 186.8 %copy-start.31 = (f32[1536]{0:T(1024)S(1)}, f32[1536]{0:T(1024)}, u32[]{:S(2)}) copy-start(f32[1536]{0:T(1024)} %get-tuple-element.659) | copy-start | bytes 18436
  943.6 187.0 %copy-start.50 = (f32[24]{0:T(128)S(1)}, f32[24]{0:T(128)}, u32[]{:S(2)}) copy-start(f32[24]{0:T(128)} %param.28) | copy-start | bytes 292
  943.6 227.0 %copy-start.36 = (f32[1536]{0:T(1024)S(1)}, f32[1536]{0:T(1024)}, u32[]{:S(2)}) copy-start(f32[1536]{0:T(1024)} %get-tuple-element.588) | copy-start | bytes 18436
  977.2 281.6 %all-to-all-start.3 = ((bf16[16,2,24576]{2,1,0:T(2,128)(2,1)}), bf16[16,2,24576]{2,1,0:T(2,128)(2,1)S(1)}, u32[]{:S(2)}, u32[]{:S(2)}) async-start(bf16[16,2,24576]{2,1,0:T(2,128)(2,1)} %reshape.519), calls=%async_computation.3 | async-start | bytes 3145728 | tf_op jit(solution)/shard_map/all_to_all | solution.py:279
  1004.6 241.9 %reduce-scatter.10.cloned.1.call-start = ((), (), s32[]{:S(2)}) async-start(), calls=%async_computation.11 | async-start | bytes 974848
  1006.1 269.6 %all-reduce.24.cloned.1.call-start = ((), (), s32[]{:S(2)}) async-start(), calls=%async_computation.12 | async-start | bytes 1916928 | tf_op jit(solution)/shard_map/psum | solution.py:283
  (36 other events, 436.0 us)
Sparse Core Ops, SparseCore 0:
  10.8 132.4 all-gather.3
  146.1 62.0 all-gather.5
  529.4 135.1 reduce-scatter.7
  897.3 232.9 reduce-scatter.5
  1133.0 76.8 reduce-scatter.9
  1212.3 15.8 all-reduce.23
where the time goes:
time: 1300 us; the launch traced here: 1290 us
  local copies, waits for them, and re-layouts  440 us (34%)
  blocking collectives  336 us (26%)
  matrix products  164 us (13%)
  other arithmetic  146 us (11%)
  waiting for transfers between devices  144 us (11%)
  starting transfers between devices  35.8 us (3%)
  between operations  19.1 us (1%)
    dynamic_update_slice x16, local copies, waits for them, and re-layouts, forward_seq(): final_state, kept = lax.scan(block_forward, start, blocks)  295 us
    unnamed x2, blocking collectives  192 us
    reduce_scatter x1, waiting for transfers between devices, on_device(): lax.psum_scatter(summed[1], 'shard', scatter_dimension=0, tiled=True)  122 us
    all_to_all x1, blocking collectives, on_device(): lax.all_to_all(sent_tokens, 'shard', split_axis=0, concat_axis=2, tiled=T...  65.5 us
    unnamed x131, local copies, waits for them, and re-layouts  55.2 us
    psum x1, blocking collectives, on_device(): lax.psum((head_terms[0], head_terms[1], head_terms[2]), ('rep', 'shard'))  40 us
    another operation x34, other arithmetic  37.8 us
    all_gather x1, blocking collectives, on_device(): lax.all_gather(conv_weight, 'shard', axis=0, tiled=True)  35.7 us
  transfers between devices with their start and end apart: 9, of which 2 were waited for; matrix products, arithmetic and copies ran while one was open for 55% of the time, Pallas kernels for 0%

commit v1 on v0

--- a/solution.py
+++ b/solution.py
@@ -11,6 +11,16 @@
 DI = 1536
 XBC = 1792
 epsilon = 1e-05
+
+
+def fill_pages_up(my_data):
+    u_next = jnp.concatenate(
+        lax.all_to_all(
+            jnp.stack(jnp.split(my_data, lax.axis_size("shard"), axis=0)), "shard", 0, 0
+        ),
+        axis=2,
+    )
+    return u_next
 
 
 def decay_terms(log_block, step_block):
@@ -240,7 +250,7 @@
     sent_tokens = jnp.take(tokens, inverse, axis=0).reshape(peers, 1, piece, width)
     sent_cot = jnp.take(cotangent, inverse, axis=0).reshape(peers, 1, piece, width)
     got_tokens, got_cot = (
-        lax.all_to_all(sent_tokens, "shard", split_axis=0, concat_axis=2, tiled=True),
+        fill_pages_up(sent_tokens),
         lax.all_to_all(sent_cot, "shard", split_axis=0, concat_axis=2, tiled=True),
     )
     seq_len = got_tokens.shape[2]

time: 1300 us -> 1300 us (level)
    unnamed x131 -> x149, local copies, waits for them, and re-layouts: 55.2 us -> 54.7 us
where the time goes in v1:
time: 1300 us; the launch traced here: 1290 us
  local copies, waits for them, and re-layouts  441 us (34%)
  blocking collectives  337 us (26%)
  matrix products  163 us (13%)
  other arithmetic  146 us (11%)
  waiting for transfers between devices  145 us (11%)
  starting transfers between devices  37 us (3%)
  between operations  19.3 us (1%)
    dynamic_update_slice x16, local copies, waits for them, and re-layouts, forward_seq(): final_state, kept = lax.scan(block_forward, start, blocks)  295 us
    unnamed x2, blocking collectives  192 us
    reduce_scatter x1, waiting for transfers between devices, on_device(): lax.psum_scatter(summed[1], 'shard', scatter_dimension=0, tiled=True)  123 us
    all_to_all x1, blocking collectives, fill_pages_up(): lax.all_to_all(jnp.stack(jnp.split(my_data, lax.axis_size('shard'), axis=...  66.4 us
    unnamed x149, local copies, waits for them, and re-layouts  54.7 us
    psum x1, blocking collectives, on_device(): lax.psum((head_terms[0], head_terms[1], head_terms[2]), ('rep', 'shard'))  40.1 us
    another operation x34, other arithmetic  37.8 us
    all_gather x1, blocking collectives, on_device(): lax.all_gather(conv_weight, 'shard', axis=0, tiled=True)  35.7 us
  transfers between devices with their start and end apart: 9, of which 2 were waited for; matrix products, arithmetic and copies ran while one was open for 55% of the time, Pallas kernels for 0%

profile of v1, /device:TPU:0, one launch (start us, length us, event | category | flops | bytes accessed | tf_op | source)
XLA Modules:
  0.0 1289.6 jit_solution(7078022193060803589)
XLA Ops:
  14.5 66.4 %all_to_all.38 = bf16[16,1,1,64,768]{4,3,2,1,0:T(8,128)(2,1)S(1)} all-to-all(bf16[16,1,1,64,768]{4,3,2,1,0:T(8,128)(2,1)S(1)} %fusion.126), channel_id=1, replica_groups=mesh['rep'=2,'shard'=16] {'shard'}, dimensions={0} | all-to-all | bytes 3145728 | tf_op jit(solution)/shard_map/all_to_all | solution.py:18
  89.8 116.5 %all-reduce.21 = (bf16[768]{0:T(1024)(128)(2,1)S(1)}, bf16[1792]{0:T(1024)(128)(2,1)S(1)}, bf16[1536]{0:T(1024)(128)(2,1)S(1)}) all-reduce(bf16[768]{0:T(1024)(128)(2,1)S(1)} %dynamic-update-slice, bf16[1792]{0:T(1024)(128)(2,1)S(1)} %dynamic-update-slice.1, ...), channel_id=1, replica_groups=mesh['rep'=2,'shard'=16] {'shard'}, use_global_device_ids=true, to_apply=%add.11 | all-reduce | flops 4096 | bytes 16384
  206.4 35.7 %all-gather = bf16[16,112,4]{1,2,0:T(4,128)(2,1)S(1)} all-gather(bf16[1,112,4]{1,2,0:T(4,128)(2,1)S(1)} %bitcast.521), channel_id=1, replica_groups=mesh['rep'=2,'shard'=16] {'shard'}, dimensions={0}, use_global_device_ids=true | all-gather | bytes 15232 | tf_op jit(solution)/shard_map/all_gather | solution.py:261
  297.7 182.0 %while.40 = (s32[]{:T(128)}, f32[24,64,128]{2,1,0:T(8,128)S(1)}, f32[4,256,24,64]{1,0,3,2:T(4,128)}, f32[4,24,64,128]{3,2,1,0:T(8,128)}, f32[4,256,24]{1,2,0:T(8...) while((s32[]{:T(128)}, f32[24,64,128]{2,1,0:T(8,128)S(1)}, ...), condition=%wide.region_5.7_spmd.clone, body=%wide.region_2.0_spmd.clone.sunk | while | flops 432687168 | bytes 17880888 | solution.py:163
  306.2 34.5 %dynamic_update_slice.73 = f32[4,256,24,64]{1,0,3,2:T(4,128)} dynamic-update-slice(f32[4,256,24,64]{1,0,3,2:T(4,128)} %get-tuple-element.896, f32[1,256,24,64]{1,0,3,2:T(1,128)S(1)} %copy.357, s32[]{:T(128)} %get-tuple-element.894, s32[]{:T(128)} %constant.126.clone.1..sunk, s32[]{:T(128)} %constant.126.clone.1..sunk, s32[]{:T(128)} %constant.126.clone.1..sunk) | dynamic-update-slice | bytes 3145732 | tf_op jit(solution)/shard_map/while/body/jit(dynamic_update_index_in_dim)/dynamic_update_slice | solution.py:163
  351.7 34.5 %dynamic_update_slice.73 = f32[4,256,24,64]{1,0,3,2:T(4,128)} dynamic-update-slice(f32[4,256,24,64]{1,0,3,2:T(4,128)} %get-tuple-element.896, f32[1,256,24,64]{1,0,3,2:T(1,128)S(1)} %copy.357, s32[]{:T(128)} %get-tuple-element.894, s32[]{:T(128)} %constant.126.clone.1..sunk, s32[]{:T(128)} %constant.126.clone.1..sunk, s32[]{:T(128)} %constant.126.clone.1..sunk) | dynamic-update-slice | bytes 3145732 | tf_op jit(solution)/shard_map/while/body/jit(dynamic_update_index_in_dim)/dynamic_update_slice | solution.py:163
  397.1 34.5 %dynamic_update_slice.73 = f32[4,256,24,64]{1,0,3,2:T(4,128)} dynamic-update-slice(f32[4,256,24,64]{1,0,3,2:T(4,128)} %get-tuple-element.896, f32[1,256,24,64]{1,0,3,2:T(1,128)S(1)} %copy.357, s32[]{:T(128)} %get-tuple-element.894, s32[]{:T(128)} %constant.126.clone.1..sunk, s32[]{:T(128)} %constant.126.clone.1..sunk, s32[]{:T(128)} %constant.126.clone.1..sunk) | dynamic-update-slice | bytes 3145732 | tf_op jit(solution)/shard_map/while/body/jit(dynamic_update_index_in_dim)/dynamic_update_slice | solution.py:163
  442.6 34.5 %dynamic_update_slice.73 = f32[4,256,24,64]{1,0,3,2:T(4,128)} dynamic-update-slice(f32[4,256,24,64]{1,0,3,2:T(4,128)} %get-tuple-element.896, f32[1,256,24,64]{1,0,3,2:T(1,128)S(1)} %copy.357, s32[]{:T(128)} %get-tuple-element.894, s32[]{:T(128)} %constant.126.clone.1..sunk, s32[]{:T(128)} %constant.126.clone.1..sunk, s32[]{:T(128)} %constant.126.clone.1..sunk) | dynamic-update-slice | bytes 3145732 | tf_op jit(solution)/shard_map/while/body/jit(dynamic_update_index_in_dim)/dynamic_update_slice | solution.py:163
  507.4 14.3 %multiply_reduce_fusion.7 = (f32[1536]{0:T(1024)}, f32[1024,1536]{0,1:T(8,128)}, bf16[1024,1536]{0,1:T(8,128)(2,1)}) fusion(f32[1024,1792]{0,1:T(8,128)} %copy-done.2, f32[1024,3352]{0,1:T(8,128)} %fusion.156, f32[1024,1536]{0,1:T(8,128)S(1)} %copy-done.8, f32[1024]{0:T(1024)S(1)} %multiply_multiply_fusion.1, f32[1024]{0:T(1024)S(1)} %fusion.143, ...), kind=kLoop, calls=%fused_computation.179 | loop fusion | flops 34601472 | bytes 40921088 | tf_op jit(solution)/shard_map/transpose(jvp())/reduce_sum | solution.py:62
  536.9 292.3 %while.41 = (s32[]{:T(128)}, f32[24,64,128]{2,1,0:T(8,128)S(1)}, f32[4,256,24,64]{1,0,3,2:T(4,128)}, f32[4,256,128]{2,1,0:T(8,128)}, f32[4,256,128]{2,1,0:T(8,12...) while((s32[]{:T(128)}, f32[24,64,128]{2,1,0:T(8,128)S(1)}, ...), condition=%wide.region_21.23_spmd.clone, body=%wide.region_8.22_spmd.clone.sunk | while | flops 998139968 | bytes 33770432 | solution.py:187
  563.1 34.8 %dynamic_update_slice.76 = f32[4,256,24,64]{1,0,3,2:T(4,128)} dynamic-update-slice(f32[4,256,24,64]{1,0,3,2:T(4,128)} %get-tuple-element.938, f32[1,256,24,64]{1,0,3,2:T(1,128)} %copy.370, s32[]{:T(128)S(6)} %sub.232, s32[]{:T(128)} %constant.126.clone.1..sunk.1, s32[]{:T(128)} %constant.126.clone.1..sunk.1, s32[]{:T(128)} %constant.126.clone.1..sunk.1) | dynamic-update-slice | bytes 3145732 | tf_op jit(solution)/shard_map/while/body/jit(dynamic_update_index_in_dim)/dynamic_update_slice | solution.py:163
  636.2 34.8 %dynamic_update_slice.76 = f32[4,256,24,64]{1,0,3,2:T(4,128)} dynamic-update-slice(f32[4,256,24,64]{1,0,3,2:T(4,128)} %get-tuple-element.938, f32[1,256,24,64]{1,0,3,2:T(1,128)} %copy.370, s32[]{:T(128)S(6)} %sub.232, s32[]{:T(128)} %constant.126.clone.1..sunk.1, s32[]{:T(128)} %constant.126.clone.1..sunk.1, s32[]{:T(128)} %constant.126.clone.1..sunk.1) | dynamic-update-slice | bytes 3145732 | tf_op jit(solution)/shard_map/while/body/jit(dynamic_update_index_in_dim)/dynamic_update_slice | solution.py:163
  709.2 34.7 %dynamic_update_slice.76 = f32[4,256,24,64]{1,0,3,2:T(4,128)} dynamic-update-slice(f32[4,256,24,64]{1,0,3,2:T(4,128)} %get-tuple-element.938, f32[1,256,24,64]{1,0,3,2:T(1,128)} %copy.370, s32[]{:T(128)S(6)} %sub.232, s32[]{:T(128)} %constant.126.clone.1..sunk.1, s32[]{:T(128)} %constant.126.clone.1..sunk.1, s32[]{:T(128)} %constant.126.clone.1..sunk.1) | dynamic-update-slice | bytes 3145732 | tf_op jit(solution)/shard_map/while/body/jit(dynamic_update_index_in_dim)/dynamic_update_slice | solution.py:163
  782.2 34.7 %dynamic_update_slice.76 = f32[4,256,24,64]{1,0,3,2:T(4,128)} dynamic-update-slice(f32[4,256,24,64]{1,0,3,2:T(4,128)} %get-tuple-element.938, f32[1,256,24,64]{1,0,3,2:T(1,128)} %copy.370, s32[]{:T(128)S(6)} %sub.232, s32[]{:T(128)} %constant.126.clone.1..sunk.1, s32[]{:T(128)} %constant.126.clone.1..sunk.1, s32[]{:T(128)} %constant.126.clone.1..sunk.1) | dynamic-update-slice | bytes 3145732 | tf_op jit(solution)/shard_map/while/body/jit(dynamic_update_index_in_dim)/dynamic_update_slice | solution.py:163
  845.1 19.0 %multiply_reduce_fusion.4 = (f32[1792]{0:T(1024)S(1)}, f32[1792]{0:T(1024)S(1)}, f32[1792]{0:T(1024)S(1)}, f32[1792]{0:T(1024)S(1)}, f32[1792]{0:T(1024)S(1)}, /*index=5*/f32[1024,1792]{0,1:T(8,128)S(1)}) fusion(f32[1024,1792]{0,1:T(8,128)} %copy-done.3, f32[1024,3352]{0,1:T(8,128)} %fusion.156, f32[1024,1792]{0,1:T(8,128)} %get-tuple-element.668, ...), kind=kLoop, calls=%fused_computation.169 | loop fusion | flops 36691200 | bytes 36736000 | tf_op jit(solution)/shard_map/transpose(jvp())/reduce_sum | solution.py:52
  872.6 12.1 fusion.103
  884.8 12.9 %fusion.119 = f32[768,3352]{1,0:T(8,128)} fusion(bf16[1024,768]{1,0:T(8,128)(2,1)S(1)} %copy-done.13, bf16[1024,24]{0,1:T(8,128)(2,1)S(1)} %get-tuple-element.662, bf16[1024,1792]{0,1:T(8,128)(2,1)} %fusion.103, bf16[1024,1536]{0,1:T(8,128)(2,1)} %get-tuple-element.685), kind=kOutput, calls=%fused_computation.210 | convolution fusion | flops 5292834816 | bytes 18735104 | tf_op jit(solution)/shard_map/ti,tj->ij/dot_general | solution.py:209
  910.1 11.7 reduce.21
  944.1 11.4 reduce.20
  956.9 20.6 %all-to-all-done.1 = bf16[16,2,24576]{2,1,0:T(2,128)(2,1)S(1)} async-done(((bf16[16,2,24576]{2,1,0:T(2,128)(2,1)}), bf16[16,2,24576]{2,1,0:T(2,128)(2,1)S(1)}, u32[]{:S(2)}, u32[]{:S(2)}) %all-to-all-start.1) | async-done | bytes 1572896 | tf_op jit(solution)/shard_map/all_to_all | solution.py:288
  977.6 28.4 %all-to-all-start.3 = ((bf16[16,2,24576]{2,1,0:T(2,128)(2,1)}), bf16[16,2,24576]{2,1,0:T(2,128)(2,1)S(1)}, u32[]{:S(2)}, u32[]{:S(2)}) async-start(bf16[16,2,24576]{2,1,0:T(2,128)(2,1)} %reshape.540), calls=%async_computation.3 | async-start | bytes 3145728 | tf_op jit(solution)/shard_map/all_to_all | solution.py:289
  1007.5 122.9 %reduce-scatter.6.cloned.1.call-done = f32[48,3352]{1,0:T(8,128)} async-done(((f32[768,3352]{1,0:T(8,128)}), f32[48,3352]{1,0:T(8,128)}) %reduce-scatter.6.cloned.1.call-update) | async-done | bytes 643600 | tf_op jit(solution)/shard_map/reduce_scatter | solution.py:306
  1132.5 40.1 %all-reduce.17 = (f32[24]{0:T(128)}, f32[24]{0:T(128)}, f32[24]{0:T(128)}) all-reduce(f32[24]{0:T(128)S(1)} %get-tuple-element.661, f32[24]{0:T(128)S(1)} %negate_multiply_fusion, f32[24]{0:T(128)S(1)} %reduce_sum.344), channel_id=1, replica_groups=mesh['rep'=2,'shard'=16] {'rep','shard'}, use_global_device_ids=true, to_apply=%region_38.40 | all-reduce | flops 72 | bytes 576 | tf_op jit(solution)/shard_map/psum | solution.py:312
  1172.6 75.3 %all-reduce.18 = (f32[768]{0:T(1024)S(1)}, f32[1792]{0:T(1024)S(1)}, f32[1536]{0:T(1024)S(1)}) all-reduce(f32[768]{0:T(1024)S(1)} %get-tuple-element.592, f32[1792]{0:T(1024)S(1)} %get-tuple-element.590, f32[1536]{0:T(1024)S(1)} %copy-done.38), channel_id=2, replica_groups=mesh['rep'=2,'shard'=16] {'shard'}, use_global_device_ids=true, to_apply=%region_25.27.clone | all-reduce | flops 4096 | bytes 32768
  (460 shorter events, 404.8 us)
Async XLA Ops:
  7.2 241.6 %all-gather.4.cloned.1.call-start = ((), (), s32[]{:S(2)}) async-start(), calls=%async_computation.7 | async-start | bytes 5640192 | tf_op jit(solution)/shard_map/all_gather | solution.py:260
  14.4 72.1 %copy-start.43 = (u32[32]{0:T(128)S(1)}, u32[32]{0:T(128)}, u32[]{:S(2)}) copy-start(u32[32]{0:T(128)} %constant.162) | copy-start | bytes 388
  14.5 74.6 %copy-start.46 = (bf16[112]{0:T(256)(128)(2,1)S(1)}, bf16[112]{0:T(256)(128)(2,1)}, u32[]{:S(2)}) copy-start(bf16[112]{0:T(256)(128)(2,1)} %param.26) | copy-start | bytes 676
  14.5 74.9 %copy-start.47 = (bf16[96]{0:T(256)(128)(2,1)S(1)}, bf16[96]{0:T(256)(128)(2,1)}, u32[]{:S(2)}) copy-start(bf16[96]{0:T(256)(128)(2,1)} %param.30) | copy-start | bytes 580
  14.5 75.1 %copy-start.48 = (bf16[48]{0:T(256)(128)(2,1)S(1)}, bf16[48]{0:T(256)(128)(2,1)}, u32[]{:S(2)}) copy-start(bf16[48]{0:T(256)(128)(2,1)} %param.23) | copy-start | bytes 292
  14.5 191.9 %copy-start.44 = (bf16[112,4]{0,1:T(4,128)(2,1)S(1)}, bf16[112,4]{0,1:T(4,128)(2,1)}, u32[]{:S(2)}) copy-start(bf16[112,4]{0,1:T(4,128)(2,1)} %param.25) | copy-start | bytes 2692
  14.5 227.6 %copy-start.45 = (f32[24]{0:T(128)S(1)}, f32[24]{0:T(128)}, u32[]{:S(2)}) copy-start(f32[24]{0:T(128)} %param.29) | copy-start | bytes 292
  14.5 227.8 %copy-start.49 = (s32[1,16]{1,0:T(1,128)S(1)}, s32[1,16]{1,0:T(1,128)}, u32[]{:S(2)}) copy-start(s32[1,16]{1,0:T(1,128)} %param.21) | copy-start | bytes 196
  14.5 229.1 %copy-start.51 = (f32[24]{0:T(128)S(1)}, f32[24]{0:T(128)}, u32[]{:S(2)}) copy-start(f32[24]{0:T(128)} %param.28) | copy-start | bytes 292
  80.9 164.8 %copy-start.5 = (bf16[16,1,1,64,768]{4,3,2,1,0:T(8,128)(2,1)}, bf16[16,1,1,64,768]{4,3,2,1,0:T(8,128)(2,1)S(1)}, u32[]{:S(2)}) copy-start(bf16[16,1,1,64,768]{4,3,2,1,0:T(8,128)(2,1)S(1)} %all_to_all.38) | copy-start | bytes 4718596
  80.9 164.9 %all-to-all-start.2 = ((bf16[16,1,64,768]{3,2,1,0:T(8,128)(2,1)}), bf16[16,1,64,768]{3,2,1,0:T(8,128)(2,1)}, u32[]{:S(2)}, u32[]{:S(2)}) async-start(bf16[16,1,64,768]{3,2,1,0:T(8,128)(2,1)} %get-tuple-element.697), calls=%async_computation.2 | async-start | bytes 3145728 | tf_op jit(solution)/shard_map/all_to_all | solution.py:254
  85.6 413.9 %all-gather.6.cloned.1.call-start = ((), (), s32[]{:S(2)}) async-start(), calls=%async_computation.8 | async-start | bytes 2506752 | tf_op jit(solution)/shard_map/all_gather | solution.py:264
  86.4 921.1 %reduce-scatter.8.cloned.1.call-start = ((), (), s32[]{:S(2)}) async-start(), calls=%async_computation.10 | async-start | bytes 5013504 | tf_op jit(solution)/shard_map/reduce_scatter | solution.py:310
  242.3 265.1 %copy-start.31 = (f32[1536]{0:T(1024)}, f32[1536]{0:T(1024)S(1)}, u32[]{:S(2)}) copy-start(f32[1536]{0:T(1024)S(1)} %convert_element_type.162) | copy-start | bytes 18436
  243.7 47.6 %copy-start.41 = (f32[24]{0:T(128)}, f32[24]{0:T(128)S(1)}, u32[]{:S(2)}) copy-start(f32[24]{0:T(128)S(1)} %exponential_negate_fusion) | copy-start | bytes 292
  529.8 600.5 %reduce-scatter.6.cloned.1.call-start = ((), (), s32[]{:S(2)}) async-start(), calls=%async_computation.9 | async-start | bytes 11280384 | tf_op jit(solution)/shard_map/reduce_scatter | solution.py:306
  923.1 54.4 %all-to-all-start.1 = ((bf16[16,2,24576]{2,1,0:T(2,128)(2,1)}), bf16[16,2,24576]{2,1,0:T(2,128)(2,1)S(1)}, u32[]{:S(2)}, u32[]{:S(2)}) async-start(bf16[16,2,24576]{2,1,0:T(2,128)(2,1)} %reshape.538), calls=%async_computation.1 | async-start | bytes 3145728 | tf_op jit(solution)/shard_map/all_to_all | solution.py:288
  956.9 175.4 %copy-start.50 = (s32[1,16]{1,0:T(1,128)S(1)}, s32[1,16]{1,0:T(1,128)}, u32[]{:S(2)}) copy-start(s32[1,16]{1,0:T(1,128)} %param.22) | copy-start | bytes 196
  956.9 175.4 %copy-start.33 = (f32[1536]{0:T(1024)S(1)}, f32[1536]{0:T(1024)}, u32[]{:S(2)}) copy-start(f32[1536]{0:T(1024)} %get-tuple-element.659) | copy-start | bytes 18436
  956.9 175.6 %copy-start.52 = (f32[24]{0:T(128)S(1)}, f32[24]{0:T(128)}, u32[]{:S(2)}) copy-start(f32[24]{0:T(128)} %param.28) | copy-start | bytes 292
  956.9 215.7 %copy-start.38 = (f32[1536]{0:T(1024)S(1)}, f32[1536]{0:T(1024)}, u32[]{:S(2)}) copy-start(f32[1536]{0:T(1024)} %get-tuple-element.588) | copy-start | bytes 18436
  977.6 282.9 %all-to-all-start.3 = ((bf16[16,2,24576]{2,1,0:T(2,128)(2,1)}), bf16[16,2,24576]{2,1,0:T(2,128)(2,1)S(1)}, u32[]{:S(2)}, u32[]{:S(2)}) async-start(bf16[16,2,24576]{2,1,0:T(2,128)(2,1)} %reshape.540), calls=%async_computation.3 | async-start | bytes 3145728 | tf_op jit(solution)/shard_map/all_to_all | solution.py:289
  1006.0 242.2 %reduce-scatter.10.cloned.1.call-start = ((), (), s32[]{:S(2)}) async-start(), calls=%async_computation.11 | async-start | bytes 974848
  1007.4 271.5 %all-reduce.24.cloned.1.call-start = ((), (), s32[]{:S(2)}) async-start(), calls=%async_computation.12 | async-start | bytes 1916928 | tf_op jit(solution)/shard_map/psum | solution.py:293
  (38 other events, 373.4 us)
Sparse Core Ops, SparseCore 0:
  10.8 133.4 all-gather.3
  147.1 61.9 all-gather.5
  529.9 134.9 reduce-scatter.7
  897.8 232.4 reduce-scatter.5
  1133.0 76.9 reduce-scatter.9
  1212.4 15.9 all-reduce.23
